TPU v7x, 512 devices: a whole 4x8x8 slice. The times are simulated.
512 devices in a mesh: rows: 32 (over x, z), cols: 16 (over y, core).
Axes of the slice: x: 4, y: 8, z: 8, core: 2. Of those that a mesh axis runs over, the one named last changes fastest.
Arguments:
- features: bfloat16 [768, 512, 2048], P(None, 'rows', 'cols'), may hold values from -6 to 6
- labels: int32 [512, 2048], P('rows', 'cols'), may hold values from 0 to 15
- w_input: bfloat16 [128, 768], replicated, may hold values from -0.21875 to 0.21875
- w_dilate4: bfloat16 [128, 1152], replicated, may hold values from -0.1875 to 0.1875
- w_dilate8: bfloat16 [128, 1152], replicated, may hold values from -0.1875 to 0.1875
- w_classes: bfloat16 [16, 128], replicated, may hold values from -0.5 to 0.5
Outputs:
- grad_input: float32 [128, 768], replicated
- grad_dilate4: float32 [128, 1152], replicated
- grad_dilate8: float32 [128, 1152], replicated
- grad_classes: float32 [16, 128], replicated
All inputs are finite; a program needn't handle non-finite values.
Results may differ from a plain program's by a relative error of at most 0.006.
Values may be sent and summed in bfloat16 or wider, within the bound.
No kernel may reach another device: no remote copies, remote signals or barrier semaphores. Data moves between devices by JAX's collectives and lax.ppermute only.
A program may use at most 128 MiB of HBM per device.

v0:
```python
import jax
import jax.numpy as jnp
from jax import lax
from jax.sharding import PartitionSpec as P

loss_weight = 0.03125


def extended(shard, sides, width):
    for axis, dim in sides:
        count, length = (lax.axis_size(axis), shard.shape[dim])
        up = [(i, (i + 1) % count) for i in range(count - 1)]
        down = [(j, i) for i, j in up]
        last = lax.slice_in_dim(shard, length - width, length, axis=dim)
        first = lax.slice_in_dim(shard, 0, width, axis=dim)
        before = lax.ppermute(last, axis, up)
        after = lax.ppermute(first, axis, down)
        shard = jnp.concatenate([before, shard, after], axis=dim)
    return shard


def smooth(value):
    return value * jax.nn.sigmoid(value)


def slope(value):
    sig = jax.nn.sigmoid(value)
    return sig * (1.0 + value * (1.0 - sig))


def gather_taps(padded, dilation, anchor, sign, out_rows, out_cols):
    pieces = []
    for tap in range(9):
        top = anchor + sign * (tap // 3 - 1) * dilation
        left = anchor + sign * (tap % 3 - 1) * dilation
        pieces.append(padded[:, top : top + out_rows, left : left + out_cols])
    stacked = jnp.concatenate(pieces, 0)
    return stacked.reshape(stacked.shape[0], out_rows * out_cols)


def pixel_contract(left, right):
    return lax.dot_general(
        left, right, (((1,), (1,)), ((), ())), preferred_element_type=jnp.float32
    )


def flipped(weight):
    chans = weight.shape[0]
    return weight.reshape(chans, 9, chans).transpose(2, 1, 0).reshape(chans, 9 * chans)


def local(features, labels, w_input, w_dilate4, w_dilate8, w_classes):
    chans = features.shape[0]
    rows = features.shape[1]
    cols = features.shape[2]
    pixels = rows * cols
    middle = w_input.shape[0]
    classes = w_classes.shape[0]
    flat = features.reshape(chans, pixels)
    a1 = jnp.dot(w_input, flat, preferred_element_type=jnp.float32)
    h1 = smooth(a1).astype(jnp.bfloat16).reshape(middle, rows, cols)
    h1_pad = extended(h1, (("rows", 1), ("cols", 2)), 4)
    a2 = jnp.dot(
        w_dilate4, gather_taps(h1_pad, 4, 4, 1, rows, cols), preferred_element_type=jnp.float32
    )
    h2 = smooth(a2).astype(jnp.bfloat16).reshape(middle, rows, cols)
    h2_pad = extended(h2, (("rows", 1), ("cols", 2)), 8)
    h2_taps = gather_taps(h2_pad, 8, 8, 1, rows, cols)
    a3 = jnp.dot(w_dilate8, h2_taps, preferred_element_type=jnp.float32)
    h3 = smooth(a3).astype(jnp.bfloat16)
    logits = jnp.dot(w_classes, h3, preferred_element_type=jnp.float32)
    expo = jnp.exp(logits)
    prob = expo / jnp.sum(expo, axis=0, keepdims=True)
    onehot = (labels.reshape(1, pixels) == jnp.arange(classes, dtype=jnp.int32)[:, None]).astype(
        jnp.float32
    )
    g4 = (loss_weight * (prob - onehot)).astype(jnp.bfloat16)
    grad_classes = pixel_contract(g4, h3)
    back3 = lax.dot_general(
        w_classes, g4, (((0,), (0,)), ((), ())), preferred_element_type=jnp.float32
    )
    g3 = (back3 * slope(a3)).astype(jnp.bfloat16)
    grad_dilate8 = pixel_contract(g3, h2_taps)
    g3_grid = g3.reshape(middle, rows, cols)
    g3_pad = extended(g3_grid, (("rows", 1), ("cols", 2)), 8)
    back2 = jnp.dot(
        flipped(w_dilate8),
        gather_taps(g3_pad, 8, 8, -1, rows, cols),
        preferred_element_type=jnp.float32,
    )
    g2 = (back2 * slope(a2)).astype(jnp.bfloat16)
    g2_grid = g2.reshape(middle, rows, cols)
    g2_pad = extended(g2_grid, (("rows", 1), ("cols", 2)), 4)
    grad_dilate4 = pixel_contract(g2, gather_taps(h1_pad, 4, 4, 1, rows, cols))
    back1 = jnp.dot(
        flipped(w_dilate4),
        gather_taps(g2_pad, 4, 4, -1, rows, cols),
        preferred_element_type=jnp.float32,
    )
    g1 = (back1 * slope(a1)).astype(jnp.bfloat16)
    grad_input = pixel_contract(g1, flat)
    grad_input, grad_dilate4, grad_dilate8, grad_classes = lax.psum(
        (grad_input, grad_dilate4, grad_dilate8, grad_classes), ("rows", "cols")
    )
    return (grad_input, grad_dilate4, grad_dilate8, grad_classes)


def solution(mesh):
    return jax.shard_map(
        local,
        mesh=mesh,
        in_specs=(P(None, "rows", "cols"), P("rows", "cols"), P(), P(), P(), P()),
        out_specs=(P(), P(), P(), P()),
        check_vma=False,
    )
```

profile of v0, /device:TPU:17, one launch (start us, length us, event | category | flops | bytes accessed | tf_op | source)
XLA Modules:
  0.0 527.5 jit_solution(8724425826203877093)
XLA Ops:
  8.1 2.5 fusion.2
  11.9 4.0 collective-permute-start
  18.1 4.7 collective-permute-done.1
  22.9 4.6 collective-permute-start.2
  34.9 2.5 copy.25
  39.3 2.5 copy.27
  41.8 2.5 copy.28
  59.0 3.3 convolution_bitcast_fusion.1
  64.0 4.7 collective-permute-start.4
  80.2 3.8 collective-permute-start.6
  89.6 2.2 pad_maximum_fusion.8
  91.8 2.4 pad_maximum_fusion
  95.4 2.1 copy.80
  109.1 2.0 copy.84
  117.8 3.4 multiply_convert_fusion
  125.8 5.2 collective-permute-start.8
  131.0 4.8 fusion.35
  136.5 3.3 collective-permute-start.10
  139.9 3.6 collective-permute-start.11
  145.8 2.3 pad_maximum_fusion.6
  148.0 2.4 maximum_maximum_fusion.1
  151.6 2.1 copy.86
  156.8 2.1 copy.87
  166.9 2.0 copy.90
  175.7 3.5 fusion.11
  181.5 4.7 collective-permute-start.12
  186.2 4.8 fusion.34
  193.0 3.9 collective-permute-start.15
  205.8 2.0 bitcast_dynamic-update-slice_fusion.6
  219.3 6.2 %fusion = f32[128,768]{1,0:T(8,128)} fusion(bf16[96,8,16,128]{3,2,1,0:T(8,128)(2,1)} %bitcast.157, bf16[1152,2048]{1,0:T(8,128)(2,1)} %bitcast_dynamic-update-slice_fusion, bf16[128,1152]{0,1:T(8,128)(2,1)} %bitcast.192, f32[128,2048]{1,0:T(8,128)S(1)} %fusion.2), kind=kOutput, calls=%fused_computation | convolution fusion | flops 1008992256 | bytes 9601024 | tf_op jit(solution)/shard_map/dot_general | solution.py:42
  225.8 106.8 %psum.31 = f32[16,128]{1,0:T(8,128)} all-reduce(f32[16,128]{1,0:T(8,128)S(1)} %fusion.16), channel_id=1, replica_groups=mesh['rows'=32,'cols'=16] {'rows','cols'}, use_global_device_ids=true, to_apply=%region_4.0 | all-reduce | flops 2048 | bytes 16384 | tf_op jit(solution)/shard_map/psum | solution.py:102
  332.6 182.4 %all-reduce.3.cloned.1.call-done = (f32[128,768]{1,0:T(8,128)}, f32[128,1152]{1,0:T(8,128)}, f32[128,1152]{1,0:T(8,128)}) async-done(((f32[128,768]{1,0:T(8,128)}, f32[128,1152]{1,0:T(8,128)}, f32[128,1152]{1,0:T(8,128)}), (f32[128,768]{1,0:T(8,128)}, f32[128,1152]{1,0:T(8,128)}, f32[128,1152]{1,0:T(8,128)})) %all-reduce.3.cloned.1.call-update) | async-done | bytes 1572880 | tf_op jit(solution)/shard_map/psum | solution.py:102
  (152 shorter events, 123.5 us)
Async XLA Ops:
  7.2 0.9 copy-start
  7.2 507.8 %all-reduce.3.cloned.1.call-start = ((), (), s32[]{:S(2)}) async-start(), calls=%async_computation | async-start | bytes 3145728 | tf_op jit(solution)/shard_map/psum | solution.py:102
  11.9 6.2 %collective-permute-start = (bf16[128,4,128]{0,1,2:T(4,128)(2,1)S(1)}, bf16[128,4,128]{0,1,2:T(4,128)(2,1)S(1)}, u32[]{:S(2)}, u32[]{:S(2)}) collective-permute-start(bf16[128,4,128]{0,1,2:T(4,128)(2,1)S(1)} %get-tuple-element.61), channel_id=1, source_target_pairs={{0,16},{16,32},{32,48},{48,64},{64,80},{80,96},{96,112},{112,128},... | collective-permute-start | bytes 393224 | tf_op jit(solution)/shard_map/ppermute | solution.py:16
  15.9 6.9 %collective-permute-start.1 = (bf16[128,4,128]{0,1,2:T(4,128)(2,1)S(1)}, bf16[128,4,128]{0,1,2:T(4,128)(2,1)S(1)}, u32[]{:S(2)}, u32[]{:S(2)}) collective-permute-start(bf16[128,4,128]{0,1,2:T(4,128)(2,1)S(1)} %get-tuple-element.62), channel_id=1, source_target_pairs={{16,0},{32,16},{48,32},{64,48},{80,64},{96,80},{112,96},{128,112},... | collective-permute-start | bytes 393224 | tf_op jit(solution)/shard_map/ppermute | solution.py:17
  22.9 9.6 %collective-permute-start.2 = (bf16[128,24,4]{0,1,2:T(8,128)(2,1)S(1)}, bf16[128,24,4]{0,1,2:T(8,128)(2,1)S(1)}, u32[]{:S(2)}, u32[]{:S(2)}) collective-permute-start(bf16[128,24,4]{0,1,2:T(8,128)(2,1)S(1)} %get-tuple-element.46), channel_id=1, source_target_pairs={{0,1},{1,2},{2,3},{3,4},{4,5},{5,6},{6,7},{7,8},{8,9},{9,10},{10,1... | collective-permute-start | bytes 73736 | tf_op jit(solution)/shard_map/ppermute | solution.py:16
  27.5 5.1 collective-permute-start.3
  64.0 13.6 %collective-permute-start.4 = (bf16[128,8,128]{0,2,1:T(8,128)(2,1)}, bf16[128,8,128]{0,2,1:T(8,128)(2,1)}, u32[]{:S(2)}, u32[]{:S(2)}) collective-permute-start(bf16[128,8,128]{0,2,1:T(8,128)(2,1)} %get-tuple-element.57), channel_id=1, source_target_pairs={{0,16},{16,32},{32,48},{48,64},{64,80},{80,96},{96,112},{112,128},... | collective-permute-start | bytes 786440 | tf_op jit(solution)/shard_map/ppermute | solution.py:16
  68.7 10.8 %collective-permute-start.5 = (bf16[128,8,128]{0,2,1:T(8,128)(2,1)}, bf16[128,8,128]{0,2,1:T(8,128)(2,1)}, u32[]{:S(2)}, u32[]{:S(2)}) collective-permute-start(bf16[128,8,128]{0,2,1:T(8,128)(2,1)} %get-tuple-element.58), channel_id=1, source_target_pairs={{16,0},{32,16},{48,32},{64,48},{80,64},{96,80},{112,96},{128,112},... | collective-permute-start | bytes 786440 | tf_op jit(solution)/shard_map/ppermute | solution.py:17
  80.2 11.5 %collective-permute-start.6 = (bf16[128,32,8]{0,2,1:T(8,128)(2,1)S(1)}, bf16[128,32,8]{0,2,1:T(8,128)(2,1)S(1)}, u32[]{:S(2)}, u32[]{:S(2)}) collective-permute-start(bf16[128,32,8]{0,2,1:T(8,128)(2,1)S(1)} %get-tuple-element.26), channel_id=1, source_target_pairs={{0,1},{1,2},{2,3},{3,4},{4,5},{5,6},{6,7},{7,8},{8,9},{9,10},{10,1... | collective-permute-start | bytes 196616 | tf_op jit(solution)/shard_map/ppermute | solution.py:16
  84.0 7.8 %collective-permute-start.7 = (bf16[128,32,8]{0,2,1:T(8,128)(2,1)S(1)}, bf16[128,32,8]{0,2,1:T(8,128)(2,1)S(1)}, u32[]{:S(2)}, u32[]{:S(2)}) collective-permute-start(bf16[128,32,8]{0,2,1:T(8,128)(2,1)S(1)} %get-tuple-element.25), channel_id=1, source_target_pairs={{1,0},{2,1},{3,2},{4,3},{5,4},{6,5},{7,6},{8,7},{9,8},{10,9},{11,1... | collective-permute-start | bytes 196616 | tf_op jit(solution)/shard_map/ppermute | solution.py:17
  94.2 5.2 copy-start.2
  117.8 3.4 copy-start.13
  117.8 3.6 copy-start.14
  121.2 1.7 copy-start.11
  122.0 13.9 %copy-start.6 = (bf16[128,2048]{1,0:T(8,128)(2,1)}, bf16[128,2048]{1,0:T(8,128)(2,1)S(1)}, u32[]{:S(2)}) copy-start(bf16[128,2048]{1,0:T(8,128)(2,1)S(1)} %fusion.9) | copy-start | bytes 1572868
  124.5 11.3 %collective-permute-start.9 = (bf16[128,8,128]{0,2,1:T(8,128)(2,1)S(1)}, bf16[128,8,128]{0,2,1:T(8,128)(2,1)S(1)}, u32[]{:S(2)}, u32[]{:S(2)}) collective-permute-start(bf16[128,8,128]{0,2,1:T(8,128)(2,1)S(1)} %get-tuple-element.54), channel_id=1, source_target_pairs={{16,0},{32,16},{48,32},{64,48},{80,64},{96,80},{112,96},{128,112},... | collective-permute-start | bytes 786440 | tf_op jit(solution)/shard_map/ppermute | solution.py:17
  125.8 10.0 %collective-permute-start.8 = (bf16[128,8,128]{0,2,1:T(8,128)(2,1)S(1)}, bf16[128,8,128]{0,2,1:T(8,128)(2,1)S(1)}, u32[]{:S(2)}, u32[]{:S(2)}) collective-permute-start(bf16[128,8,128]{0,2,1:T(8,128)(2,1)S(1)} %get-tuple-element.53), channel_id=1, source_target_pairs={{0,16},{16,32},{32,48},{48,64},{64,80},{80,96},{96,112},{112,128},... | collective-permute-start | bytes 786440 | tf_op jit(solution)/shard_map/ppermute | solution.py:16
  135.8 0.7 copy-start.8
  135.8 4.1 copy-start.9
  136.5 11.5 %collective-permute-start.10 = (bf16[128,32,8]{0,2,1:T(8,128)(2,1)S(1)}, bf16[128,32,8]{0,2,1:T(8,128)(2,1)S(1)}, u32[]{:S(2)}, u32[]{:S(2)}) collective-permute-start(bf16[128,32,8]{0,2,1:T(8,128)(2,1)S(1)} %get-tuple-element.22), channel_id=1, source_target_pairs={{1,0},{2,1},{3,2},{4,3},{5,4},{6,5},{7,6},{8,7},{9,8},{10,9},{11,1... | collective-permute-start | bytes 196616 | tf_op jit(solution)/shard_map/ppermute | solution.py:17
  139.9 8.2 %collective-permute-start.11 = (bf16[128,32,8]{0,2,1:T(8,128)(2,1)S(1)}, bf16[128,32,8]{0,2,1:T(8,128)(2,1)S(1)}, u32[]{:S(2)}, u32[]{:S(2)}) collective-permute-start(bf16[128,32,8]{0,2,1:T(8,128)(2,1)S(1)} %get-tuple-element.21), channel_id=1, source_target_pairs={{0,1},{1,2},{2,3},{3,4},{4,5},{5,6},{6,7},{7,8},{8,9},{9,10},{10,1... | collective-permute-start | bytes 196616 | tf_op jit(solution)/shard_map/ppermute | solution.py:16
  150.4 5.1 copy-start.3
  156.8 8.1 %copy-start.7 = (bf16[128,2048]{1,0:T(8,128)(2,1)S(1)}, bf16[128,2048]{1,0:T(8,128)(2,1)}, u32[]{:S(2)}) copy-start(bf16[128,2048]{1,0:T(8,128)(2,1)} %copy-done.6) | copy-start | bytes 1572868
  179.2 17.8 %copy-start.4 = (bf16[128,2048]{1,0:T(8,128)(2,1)}, bf16[128,2048]{1,0:T(8,128)(2,1)S(1)}, u32[]{:S(2)}) copy-start(bf16[128,2048]{1,0:T(8,128)(2,1)S(1)} %fusion.11) | copy-start | bytes 1572868
  180.2 10.8 %collective-permute-start.13 = (bf16[128,4,128]{0,1,2:T(4,128)(2,1)S(1)}, bf16[128,4,128]{0,1,2:T(4,128)(2,1)S(1)}, u32[]{:S(2)}, u32[]{:S(2)}) collective-permute-start(bf16[128,4,128]{0,1,2:T(4,128)(2,1)S(1)} %get-tuple-element.50), channel_id=1, source_target_pairs={{16,0},{32,16},{48,32},{64,48},{80,64},{96,80},{112,96},{128,112},... | collective-permute-start | bytes 393224 | tf_op jit(solution)/shard_map/ppermute | solution.py:17
  181.5 9.5 %collective-permute-start.12 = (bf16[128,4,128]{0,1,2:T(4,128)(2,1)S(1)}, bf16[128,4,128]{0,1,2:T(4,128)(2,1)S(1)}, u32[]{:S(2)}, u32[]{:S(2)}) collective-permute-start(bf16[128,4,128]{0,1,2:T(4,128)(2,1)S(1)} %get-tuple-element.49), channel_id=1, source_target_pairs={{0,16},{16,32},{32,48},{48,64},{64,80},{80,96},{96,112},{112,128},... | collective-permute-start | bytes 393224 | tf_op jit(solution)/shard_map/ppermute | solution.py:16
  191.0 7.7 %collective-permute-start.14 = (bf16[128,24,4]{0,1,2:T(8,128)(2,1)S(1)}, bf16[128,24,4]{0,1,2:T(8,128)(2,1)S(1)}, u32[]{:S(2)}, u32[]{:S(2)}) collective-permute-start(bf16[128,24,4]{0,1,2:T(8,128)(2,1)S(1)} %get-tuple-element.42), channel_id=1, source_target_pairs={{1,0},{2,1},{3,2},{4,3},{5,4},{6,5},{7,6},{8,7},{9,8},{10,9},{11,1... | collective-permute-start | bytes 73736 | tf_op jit(solution)/shard_map/ppermute | solution.py:17
  193.0 5.7 %collective-permute-start.15 = (bf16[128,24,4]{0,1,2:T(8,128)(2,1)S(1)}, bf16[128,24,4]{0,1,2:T(8,128)(2,1)S(1)}, u32[]{:S(2)}, u32[]{:S(2)}) collective-permute-start(bf16[128,24,4]{0,1,2:T(8,128)(2,1)S(1)} %get-tuple-element.41), channel_id=1, source_target_pairs={{0,1},{1,2},{2,3},{3,4},{4,5},{5,6},{6,7},{7,8},{8,9},{9,10},{10,1... | collective-permute-start | bytes 73736 | tf_op jit(solution)/shard_map/ppermute | solution.py:16
  201.1 8.5 %copy-start.5 = (bf16[128,2048]{1,0:T(8,128)(2,1)S(1)}, bf16[128,2048]{1,0:T(8,128)(2,1)}, u32[]{:S(2)}) copy-start(bf16[128,2048]{1,0:T(8,128)(2,1)} %copy-done.4) | copy-start | bytes 1572868
  205.8 11.7 %copy-start.10 = (bf16[128,16,128]{2,1,0:T(8,128)(2,1)S(1)}, bf16[128,16,128]{2,1,0:T(8,128)(2,1)}, u32[]{:S(2)}) copy-start(bf16[128,16,128]{2,1,0:T(8,128)(2,1)} %get-tuple-element.47) | copy-start | bytes 1572868
  219.3 6.2 %copy-start.12 = (bf16[128,2048]{1,0:T(8,128)(2,1)S(1)}, bf16[128,2048]{1,0:T(8,128)(2,1)}, u32[]{:S(2)}) copy-start(bf16[128,2048]{1,0:T(8,128)(2,1)} %copy-done.11) | copy-start | bytes 1572868
  219.3 301.3 %copy-start.1 = (bf16[128,768]{1,0:T(8,128)(2,1)S(1)}, bf16[128,768]{1,0:T(8,128)(2,1)}, u32[]{:S(2)}) copy-start(bf16[128,768]{1,0:T(8,128)(2,1)} %param.8) | copy-start | bytes 589828
Sparse Core Ops, SparseCore 0:
  225.7 289.2 all-reduce.2
where the time goes:
time: 530 us; the launch traced here: 527 us
  waiting for transfers between devices  190 us (36%)
  local copies, waits for them, and re-layouts  121 us (23%)
  blocking collectives  107 us (20%)
  starting transfers between devices  49 us (9%)
  matrix products  29.4 us (6%)
  other arithmetic  16.8 us (3%)
  between operations  14.6 us (3%)
    psum x1, waiting for transfers between devices, local(): lax.psum((grad_input, grad_dilate4, grad_dilate8, grad_classes), ('rows',...  182 us
    psum x1, blocking collectives, local(): lax.psum((grad_input, grad_dilate4, grad_dilate8, grad_classes), ('rows',...  107 us
    unnamed x69, local copies, waits for them, and re-layouts  53.3 us
    ppermute x8, starting transfers between devices, extended(): before = lax.ppermute(last, axis, up)  34.5 us
    slice x19, local copies, waits for them, and re-layouts, gather_taps(): pieces.append(padded[:, top:top + out_rows, left:left + out_cols])  28.9 us
    concatenate x16, local copies, waits for them, and re-layouts, gather_taps(): stacked = jnp.concatenate(pieces, 0)  22.5 us
    dot_general x4, matrix products, pixel_contract(): lax.dot_general(left, right, (((1,), (1,)), ((), ())), preferred_element_...  16 us
    ppermute x8, starting transfers between devices, extended(): after = lax.ppermute(first, axis, down)  14.4 us
  transfers between devices with their start and end apart: 17, of which 5 were waited for; matrix products, arithmetic and copies ran while one was open for 6% of the time, Pallas kernels for 0%

commit v1 on v0

--- a/solution.py
+++ b/solution.py
@@ -4,6 +4,12 @@
 from jax.sharding import PartitionSpec as P
 
 loss_weight = 0.03125
+
+
+def name_records(buf):
+    for k0 in ("cols", "rows"):
+        buf = lax.psum(buf, k0)
+    return buf
 
 
 def extended(shard, sides, width):
@@ -99,8 +105,8 @@
     )
     g1 = (back1 * slope(a1)).astype(jnp.bfloat16)
     grad_input = pixel_contract(g1, flat)
-    grad_input, grad_dilate4, grad_dilate8, grad_classes = lax.psum(
-        (grad_input, grad_dilate4, grad_dilate8, grad_classes), ("rows", "cols")
+    grad_input, grad_dilate4, grad_dilate8, grad_classes = name_records(
+        (grad_input, grad_dilate4, grad_dilate8, grad_classes)
     )
     return (grad_input, grad_dilate4, grad_dilate8, grad_classes)
 

time: 530 us -> 540 us (1.019)
  the two profiles are of different devices: /device:TPU:17 before, /device:TPU:8 now
where the time goes in v1:
time: 540 us; the launch traced here: 537 us
  waiting for transfers between devices  204 us (38%)
  local copies, waits for them, and re-layouts  123 us (23%)
  blocking collectives  103 us (19%)
  starting transfers between devices  45.7 us (8%)
  matrix products  29.4 us (5%)
  other arithmetic  16.7 us (3%)
  between operations  14.6 us (3%)
    psum x2, waiting for transfers between devices, name_records(): buf = lax.psum(buf, k0)  194 us
    psum x2, blocking collectives, name_records(): buf = lax.psum(buf, k0)  103 us
    unnamed x65, local copies, waits for them, and re-layouts  53.8 us
    slice x19, local copies, waits for them, and re-layouts, gather_taps(): pieces.append(padded[:, top:top + out_rows, left:left + out_cols])  31.1 us
    ppermute x8, starting transfers between devices, extended(): before = lax.ppermute(last, axis, up)  28.2 us
    concatenate x16, local copies, waits for them, and re-layouts, gather_taps(): stacked = jnp.concatenate(pieces, 0)  22.5 us
    ppermute x8, starting transfers between devices, extended(): after = lax.ppermute(first, axis, down)  17.4 us
    dot_general x4, matrix products, pixel_contract(): lax.dot_general(left, right, (((1,), (1,)), ((), ())), preferred_element_...  16 us
  transfers between devices with their start and end apart: 18, of which 7 were waited for; matrix products, arithmetic and copies ran while one was open for 6% of the time, Pallas kernels for 0%

profile of v1, /device:TPU:8, one launch (start us, length us, event | category | flops | bytes accessed | tf_op | source)
XLA Modules:
  0.0 537.3 jit_solution(17810469706531158690)
XLA Ops:
  8.1 2.5 fusion.2
  11.9 4.3 collective-permute-start
  18.9 4.8 collective-permute-done.1
  25.6 3.6 collective-permute-start.3
  34.6 2.5 copy.25
  39.1 2.5 copy.27
  41.6 2.5 copy.28
  58.7 3.3 convolution_bitcast_fusion.1
  63.8 5.0 collective-permute-start.4
  77.6 2.5 collective-permute-done.5
  82.8 3.6 collective-permute-start.7
  90.1 2.2 pad_maximum_fusion.8
  92.3 2.4 pad_maximum_fusion
  95.9 2.1 copy.80
  118.5 3.4 multiply_convert_fusion
  126.4 5.5 %collective-permute-start.8 = (bf16[128,8,128]{0,2,1:T(8,128)(2,1)S(1)}, bf16[128,8,128]{0,2,1:T(8,128)(2,1)S(1)}, u32[]{:S(2)}, u32[]{:S(2)}) collective-permute-start(bf16[128,8,128]{0,2,1:T(8,128)(2,1)S(1)} %get-tuple-element.56), channel_id=1, source_target_pairs={{0,16},{16,32},{32,48},{48,64},{64,80},{80,96},{96,112},{112,128},... | collective-permute-start | bytes 786440 | tf_op jit(solution)/shard_map/ppermute | solution.py:22
  131.9 4.8 fusion.35
  139.5 2.4 collective-permute-start.11
  144.2 2.3 pad_maximum_fusion.6
  146.5 2.4 maximum_maximum_fusion.1
  155.3 2.1 copy.87
  165.5 2.0 copy.90
  174.3 3.5 fusion.11
  180.0 5.0 collective-permute-start.12
  185.1 4.8 fusion.34
  189.9 2.9 collective-permute-start.14
  192.7 2.1 collective-permute-start.15
  221.6 6.2 %fusion = f32[128,768]{1,0:T(8,128)} fusion(bf16[96,8,16,128]{3,2,1,0:T(8,128)(2,1)} %bitcast.157, bf16[1152,2048]{1,0:T(8,128)(2,1)} %bitcast_dynamic-update-slice_fusion, bf16[128,1152]{0,1:T(8,128)(2,1)} %bitcast.192, f32[128,2048]{1,0:T(8,128)S(1)} %fusion.2), kind=kOutput, calls=%fused_computation | convolution fusion | flops 1008992256 | bytes 9601024 | tf_op jit(solution)/shard_map/dot_general | solution.py:48
  227.9 125.8 %all-reduce.7.cloned.1.call-done = (f32[128,768]{1,0:T(8,128)}, f32[128,1152]{1,0:T(8,128)}, f32[128,1152]{1,0:T(8,128)}) async-done(((f32[128,768]{1,0:T(8,128)}, f32[128,1152]{1,0:T(8,128)}, f32[128,1152]{1,0:T(8,128)}), (f32[128,768]{1,0:T(8,128)}, f32[128,1152]{1,0:T(8,128)}, f32[128,1152]{1,0:T(8,128)})) %all-reduce.7.cloned.1.call-update) | async-done | bytes 1572880 | tf_op jit(solution)/shard_map/psum | solution.py:11
  354.0 25.6 %psum.62 = f32[16,128]{1,0:T(8,128)S(1)} all-reduce(f32[16,128]{1,0:T(8,128)S(1)} %fusion.16), channel_id=1, replica_groups=mesh['rows'=32,'cols'=16] {'cols'}, use_global_device_ids=true, to_apply=%region_7.0 | all-reduce | flops 2048 | bytes 16384 | tf_op jit(solution)/shard_map/psum | solution.py:11
  379.6 77.5 %psum.63 = f32[16,128]{1,0:T(8,128)} all-reduce(f32[16,128]{1,0:T(8,128)S(1)} %psum.62), channel_id=1, replica_groups=mesh['rows'=32,'cols'=16] {'rows'}, use_global_device_ids=true, to_apply=%region_8.0 | all-reduce | flops 2048 | bytes 16384 | tf_op jit(solution)/shard_map/psum | solution.py:11
  457.0 67.8 %all-reduce.5.cloned.1.call-done = (f32[128,768]{1,0:T(8,128)}, f32[128,1152]{1,0:T(8,128)}, f32[128,1152]{1,0:T(8,128)}) async-done(((f32[128,768]{1,0:T(8,128)}, f32[128,1152]{1,0:T(8,128)}, f32[128,1152]{1,0:T(8,128)}), (f32[128,768]{1,0:T(8,128)}, f32[128,1152]{1,0:T(8,128)}, f32[128,1152]{1,0:T(8,128)})) %all-reduce.5.cloned.1.call-update) | async-done | bytes 1572880 | tf_op jit(solution)/shard_map/psum | solution.py:11
  (152 shorter events, 132.9 us)
Async XLA Ops:
  7.2 0.9 copy-start
  7.2 346.5 %all-reduce.7.cloned.1.call-start = ((), (), s32[]{:S(2)}) async-start(), calls=%async_computation.1 | async-start | bytes 3145728 | tf_op jit(solution)/shard_map/psum | solution.py:11
  11.9 7.0 %collective-permute-start = (bf16[128,4,128]{0,1,2:T(4,128)(2,1)S(1)}, bf16[128,4,128]{0,1,2:T(4,128)(2,1)S(1)}, u32[]{:S(2)}, u32[]{:S(2)}) collective-permute-start(bf16[128,4,128]{0,1,2:T(4,128)(2,1)S(1)} %get-tuple-element.64), channel_id=1, source_target_pairs={{0,16},{16,32},{32,48},{48,64},{64,80},{80,96},{96,112},{112,128},... | collective-permute-start | bytes 393224 | tf_op jit(solution)/shard_map/ppermute | solution.py:22
  16.2 7.5 %collective-permute-start.1 = (bf16[128,4,128]{0,1,2:T(4,128)(2,1)S(1)}, bf16[128,4,128]{0,1,2:T(4,128)(2,1)S(1)}, u32[]{:S(2)}, u32[]{:S(2)}) collective-permute-start(bf16[128,4,128]{0,1,2:T(4,128)(2,1)S(1)} %get-tuple-element.65), channel_id=1, source_target_pairs={{16,0},{32,16},{48,32},{64,48},{80,64},{96,80},{112,96},{128,112},... | collective-permute-start | bytes 393224 | tf_op jit(solution)/shard_map/ppermute | solution.py:23
  23.7 8.7 %collective-permute-start.2 = (bf16[128,24,4]{0,1,2:T(8,128)(2,1)S(1)}, bf16[128,24,4]{0,1,2:T(8,128)(2,1)S(1)}, u32[]{:S(2)}, u32[]{:S(2)}) collective-permute-start(bf16[128,24,4]{0,1,2:T(8,128)(2,1)S(1)} %get-tuple-element.49), channel_id=1, source_target_pairs={{0,1},{1,2},{2,3},{3,4},{4,5},{5,6},{6,7},{7,8},{8,9},{9,10},{10,1... | collective-permute-start | bytes 73736 | tf_op jit(solution)/shard_map/ppermute | solution.py:22
  25.6 6.7 %collective-permute-start.3 = (bf16[128,24,4]{0,1,2:T(8,128)(2,1)S(1)}, bf16[128,24,4]{0,1,2:T(8,128)(2,1)S(1)}, u32[]{:S(2)}, u32[]{:S(2)}) collective-permute-start(bf16[128,24,4]{0,1,2:T(8,128)(2,1)S(1)} %get-tuple-element.48), channel_id=1, source_target_pairs={{1,0},{2,1},{3,2},{4,3},{5,4},{6,5},{7,6},{8,7},{9,8},{10,9},{11,1... | collective-permute-start | bytes 73736 | tf_op jit(solution)/shard_map/ppermute | solution.py:23
  63.8 13.8 %collective-permute-start.4 = (bf16[128,8,128]{0,2,1:T(8,128)(2,1)}, bf16[128,8,128]{0,2,1:T(8,128)(2,1)}, u32[]{:S(2)}, u32[]{:S(2)}) collective-permute-start(bf16[128,8,128]{0,2,1:T(8,128)(2,1)} %get-tuple-element.60), channel_id=1, source_target_pairs={{0,16},{16,32},{32,48},{48,64},{64,80},{80,96},{96,112},{112,128},... | collective-permute-start | bytes 786440 | tf_op jit(solution)/shard_map/ppermute | solution.py:22
  68.7 11.4 %collective-permute-start.5 = (bf16[128,8,128]{0,2,1:T(8,128)(2,1)}, bf16[128,8,128]{0,2,1:T(8,128)(2,1)}, u32[]{:S(2)}, u32[]{:S(2)}) collective-permute-start(bf16[128,8,128]{0,2,1:T(8,128)(2,1)} %get-tuple-element.61), channel_id=1, source_target_pairs={{16,0},{32,16},{48,32},{64,48},{80,64},{96,80},{112,96},{128,112},... | collective-permute-start | bytes 786440 | tf_op jit(solution)/shard_map/ppermute | solution.py:23
  80.9 11.4 %collective-permute-start.6 = (bf16[128,32,8]{0,2,1:T(8,128)(2,1)S(1)}, bf16[128,32,8]{0,2,1:T(8,128)(2,1)S(1)}, u32[]{:S(2)}, u32[]{:S(2)}) collective-permute-start(bf16[128,32,8]{0,2,1:T(8,128)(2,1)S(1)} %get-tuple-element.29), channel_id=1, source_target_pairs={{0,1},{1,2},{2,3},{3,4},{4,5},{5,6},{6,7},{7,8},{8,9},{9,10},{10,1... | collective-permute-start | bytes 196616 | tf_op jit(solution)/shard_map/ppermute | solution.py:22
  82.8 9.5 %collective-permute-start.7 = (bf16[128,32,8]{0,2,1:T(8,128)(2,1)S(1)}, bf16[128,32,8]{0,2,1:T(8,128)(2,1)S(1)}, u32[]{:S(2)}, u32[]{:S(2)}) collective-permute-start(bf16[128,32,8]{0,2,1:T(8,128)(2,1)S(1)} %get-tuple-element.28), channel_id=1, source_target_pairs={{1,0},{2,1},{3,2},{4,3},{5,4},{6,5},{7,6},{8,7},{9,8},{10,9},{11,1... | collective-permute-start | bytes 196616 | tf_op jit(solution)/shard_map/ppermute | solution.py:23
  94.7 5.2 copy-start.2
  118.5 3.4 copy-start.11
  118.5 3.6 copy-start.12
  121.8 1.7 copy-start.9
  122.6 15.0 %copy-start.4 = (bf16[128,2048]{1,0:T(8,128)(2,1)}, bf16[128,2048]{1,0:T(8,128)(2,1)S(1)}, u32[]{:S(2)}) copy-start(bf16[128,2048]{1,0:T(8,128)(2,1)S(1)} %fusion.9) | copy-start | bytes 1572868
  125.1 11.6 %collective-permute-start.9 = (bf16[128,8,128]{0,2,1:T(8,128)(2,1)S(1)}, bf16[128,8,128]{0,2,1:T(8,128)(2,1)S(1)}, u32[]{:S(2)}, u32[]{:S(2)}) collective-permute-start(bf16[128,8,128]{0,2,1:T(8,128)(2,1)S(1)} %get-tuple-element.57), channel_id=1, source_target_pairs={{16,0},{32,16},{48,32},{64,48},{80,64},{96,80},{112,96},{128,112},... | collective-permute-start | bytes 786440 | tf_op jit(solution)/shard_map/ppermute | solution.py:23
  126.4 11.2 %collective-permute-start.8 = (bf16[128,8,128]{0,2,1:T(8,128)(2,1)S(1)}, bf16[128,8,128]{0,2,1:T(8,128)(2,1)S(1)}, u32[]{:S(2)}, u32[]{:S(2)}) collective-permute-start(bf16[128,8,128]{0,2,1:T(8,128)(2,1)S(1)} %get-tuple-element.56), channel_id=1, source_target_pairs={{0,16},{16,32},{32,48},{48,64},{64,80},{80,96},{96,112},{112,128},... | collective-permute-start | bytes 786440 | tf_op jit(solution)/shard_map/ppermute | solution.py:22
  136.7 0.9 copy-start.6
  137.6 2.0 copy-start.7
  137.6 8.9 %collective-permute-start.10 = (bf16[128,32,8]{0,2,1:T(8,128)(2,1)S(1)}, bf16[128,32,8]{0,2,1:T(8,128)(2,1)S(1)}, u32[]{:S(2)}, u32[]{:S(2)}) collective-permute-start(bf16[128,32,8]{0,2,1:T(8,128)(2,1)S(1)} %get-tuple-element.25), channel_id=1, source_target_pairs={{1,0},{2,1},{3,2},{4,3},{5,4},{6,5},{7,6},{8,7},{9,8},{10,9},{11,1... | collective-permute-start | bytes 196616 | tf_op jit(solution)/shard_map/ppermute | solution.py:23
  139.5 7.0 %collective-permute-start.11 = (bf16[128,32,8]{0,2,1:T(8,128)(2,1)S(1)}, bf16[128,32,8]{0,2,1:T(8,128)(2,1)S(1)}, u32[]{:S(2)}, u32[]{:S(2)}) collective-permute-start(bf16[128,32,8]{0,2,1:T(8,128)(2,1)S(1)} %get-tuple-element.24), channel_id=1, source_target_pairs={{0,1},{1,2},{2,3},{3,4},{4,5},{5,6},{6,7},{7,8},{8,9},{9,10},{10,1... | collective-permute-start | bytes 196616 | tf_op jit(solution)/shard_map/ppermute | solution.py:22
  148.9 5.2 copy-start.3
  155.3 8.1 %copy-start.5 = (bf16[128,2048]{1,0:T(8,128)(2,1)S(1)}, bf16[128,2048]{1,0:T(8,128)(2,1)}, u32[]{:S(2)}) copy-start(bf16[128,2048]{1,0:T(8,128)(2,1)} %copy-done.4) | copy-start | bytes 1572868
  178.7 11.1 %collective-permute-start.13 = (bf16[128,4,128]{0,1,2:T(4,128)(2,1)S(1)}, bf16[128,4,128]{0,1,2:T(4,128)(2,1)S(1)}, u32[]{:S(2)}, u32[]{:S(2)}) collective-permute-start(bf16[128,4,128]{0,1,2:T(4,128)(2,1)S(1)} %get-tuple-element.53), channel_id=1, source_target_pairs={{16,0},{32,16},{48,32},{64,48},{80,64},{96,80},{112,96},{128,112},... | collective-permute-start | bytes 393224 | tf_op jit(solution)/shard_map/ppermute | solution.py:23
  180.0 9.8 %collective-permute-start.12 = (bf16[128,4,128]{0,1,2:T(4,128)(2,1)S(1)}, bf16[128,4,128]{0,1,2:T(4,128)(2,1)S(1)}, u32[]{:S(2)}, u32[]{:S(2)}) collective-permute-start(bf16[128,4,128]{0,1,2:T(4,128)(2,1)S(1)} %get-tuple-element.52), channel_id=1, source_target_pairs={{0,16},{16,32},{32,48},{48,64},{64,80},{80,96},{96,112},{112,128},... | collective-permute-start | bytes 393224 | tf_op jit(solution)/shard_map/ppermute | solution.py:22
  189.9 6.9 %collective-permute-start.14 = (bf16[128,24,4]{0,1,2:T(8,128)(2,1)S(1)}, bf16[128,24,4]{0,1,2:T(8,128)(2,1)S(1)}, u32[]{:S(2)}, u32[]{:S(2)}) collective-permute-start(bf16[128,24,4]{0,1,2:T(8,128)(2,1)S(1)} %get-tuple-element.45), channel_id=1, source_target_pairs={{1,0},{2,1},{3,2},{4,3},{5,4},{6,5},{7,6},{8,7},{9,8},{10,9},{11,1... | collective-permute-start | bytes 73736 | tf_op jit(solution)/shard_map/ppermute | solution.py:23
  192.7 5.1 collective-permute-start.15
  207.0 12.8 %copy-start.8 = (bf16[128,16,128]{2,1,0:T(8,128)(2,1)S(1)}, bf16[128,16,128]{2,1,0:T(8,128)(2,1)}, u32[]{:S(2)}) copy-start(bf16[128,16,128]{2,1,0:T(8,128)(2,1)} %get-tuple-element.50) | copy-start | bytes 1572868
  221.6 132.1 %copy-start.10 = (bf16[128,2048]{1,0:T(8,128)(2,1)S(1)}, bf16[128,2048]{1,0:T(8,128)(2,1)}, u32[]{:S(2)}) copy-start(bf16[128,2048]{1,0:T(8,128)(2,1)} %copy-done.9) | copy-start | bytes 1572868
  221.6 308.9 %copy-start.1 = (bf16[128,768]{1,0:T(8,128)(2,1)S(1)}, bf16[128,768]{1,0:T(8,128)(2,1)}, u32[]{:S(2)}) copy-start(bf16[128,768]{1,0:T(8,128)(2,1)} %param.8) | copy-start | bytes 589828
  227.9 297.0 %all-reduce.5.cloned.1.call-start = ((), (), s32[]{:S(2)}) async-start(), calls=%async_computation | async-start | bytes 3145728 | tf_op jit(solution)/shard_map/psum | solution.py:11
Sparse Core Ops, SparseCore 0:
  228.0 125.6 all-reduce.6
  357.4 167.4 all-reduce.4
